TPU v7x, 32 devices: a whole 2x2x4 slice. The times are simulated.
32 devices in a mesh: tm: 4 (over x, core), chan: 8 (over z, y).
Axes of the slice: x: 2, y: 2, z: 4, core: 2. Of those that a mesh axis runs over, the one named last changes fastest.
Arguments:
- raw_blocks: bfloat16 [16, 5120, 1024], P('tm', 'chan'), may hold values from -6 to 6
- fir_taps: bfloat16 [128], replicated, may hold values from -0.5 to 0.5
- recorder_channel: int32 [5120], replicated, may hold values from 0 to 5119, as said below
- pairs: int32 [4096, 2], P('chan'), may hold values from 0 to 5119, as said below
Outputs:
- stacks: float32 [4096, 256], P('chan')
Inputs may be any that keep to these rules, and one draw needn't show every extreme that they name: `recorder_channel`: A permutation of the channels; each aligned block of 640 recorder rows holds exactly 80 channels of every range of 640 consecutive channels. `pairs`: each aligned block of 512 rows names exactly 32 distinct channels of every range of 640 consecutive channels.
All inputs are finite; a program needn't handle non-finite values.
Results may differ from a plain program's by a relative error of at most 0.0084.
Values may be sent and summed in bfloat16 or wider, within the bound.
No kernel may reach another device: no remote copies, remote signals or barrier semaphores. Data moves between devices by JAX's collectives and lax.ppermute only.
A program may use at most 128 MiB of HBM per device.

v0:
```python
import jax
import jax.numpy as jnp
from jax import lax
from jax.sharding import PartitionSpec as P

NB = 128
SMOOTH = 4


def make_fir(fir_taps, length):
    taps_n = fir_taps.shape[0]
    period = taps_n + length
    padded = jnp.concatenate([fir_taps.astype(jnp.float32), jnp.zeros((length,), jnp.float32)])
    repeated = jnp.tile(padded, length)[: length * (period - 1)].reshape(length, period - 1)[
        :, :length
    ]
    return repeated.astype(jnp.bfloat16)


def make_table(length, bin_count):
    samples = jnp.arange(length, dtype=jnp.int32)
    freqs = jnp.arange(1, bin_count + 1, dtype=jnp.int32)
    phase_idx = samples[:, None] * freqs[None, :] % length
    angles = phase_idx.astype(jnp.float32) * (2.0 * jnp.pi / length)
    return jnp.concatenate([jnp.cos(angles), -jnp.sin(angles)], axis=1).astype(jnp.bfloat16)


def make_smooth(bin_count, half_width):
    places = jnp.arange(bin_count, dtype=jnp.int32)
    band_mask = (jnp.abs(places[:, None] - places[None, :]) <= half_width).astype(jnp.float32)
    return band_mask / jnp.sum(band_mask, axis=0, keepdims=True)


def whiten(spectrum, smoother):
    bin_count = spectrum.shape[-1] // 2
    real_part = spectrum[..., :bin_count]
    imag_part = spectrum[..., bin_count:]
    magnitude = jnp.sqrt(real_part * real_part + imag_part * imag_part)
    smoothed = jnp.dot(magnitude, smoother, precision=lax.Precision.HIGHEST)
    mean_level = jnp.mean(magnitude, axis=-1, keepdims=True)
    divisor = smoothed + 0.1 * mean_level + 1e-06
    return (spectrum / jnp.concatenate([divisor, divisor], axis=-1)).astype(jnp.bfloat16)


def cross(left_rows, right_rows):
    bin_count = left_rows.shape[-1] // 2
    left_f = left_rows.astype(jnp.float32)
    right_f = right_rows.astype(jnp.float32)
    left_re, left_im = (left_f[..., :bin_count], left_f[..., bin_count:])
    right_re, right_im = (right_f[..., :bin_count], right_f[..., bin_count:])
    real_out = left_re * right_re + left_im * right_im
    imag_out = left_im * right_re - left_re * right_im
    return jnp.concatenate([real_out, imag_out], axis=-1)


def local(raw_blocks, fir_taps, recorder_channel, pairs):
    windows, ch_dev, length = raw_blocks.shape
    rows_of = jnp.argsort(recorder_channel, stable=True)
    endpoints = jnp.concatenate([pairs[:, 0], pairs[:, 1]])
    wanted_ids = jnp.take(rows_of, endpoints)
    fir_matrix = make_fir(fir_taps, length)
    dft_table = make_table(length, NB)
    smoother = make_smooth(NB, SMOOTH)
    flat_rows = raw_blocks.reshape(windows * ch_dev, length)
    filtered = jnp.dot(flat_rows, fir_matrix, preferred_element_type=jnp.float32).astype(
        jnp.bfloat16
    )
    spectrum = jnp.dot(filtered, dft_table, preferred_element_type=jnp.float32)
    whitened = whiten(spectrum, smoother).reshape(windows, ch_dev, 2 * NB)
    pair_count = pairs.shape[0]
    empty = jnp.zeros((windows, 2 * pair_count, 2 * NB), jnp.bfloat16)
    part_rows = lax.all_gather(whitened, "chan", axis=1, tiled=True)
    inside = (wanted_ids >= 0) & (wanted_ids < part_rows.shape[1])
    taken = jnp.take(part_rows, jnp.clip(wanted_ids, 0, part_rows.shape[1] - 1), axis=1)
    chosen = jnp.where(inside[None, :, None], taken, empty)
    products = cross(chosen[:, :pair_count], chosen[:, pair_count:])
    stacked = jnp.sum(products, axis=0)
    summed = lax.psum(stacked, "tm")
    return summed / (windows * lax.axis_size("tm"))


def solution(mesh):
    in_specs = (P("tm", "chan", None), P(), P(), P("chan", None))
    out_specs = P("chan", None)
    return jax.shard_map(local, mesh=mesh, in_specs=in_specs, out_specs=out_specs, check_vma=False)
```

profile of v0, /device:TPU:0, one launch (start us, length us, event | category | flops | bytes accessed | tf_op | source)
XLA Modules:
  0.0 248.1 jit_solution(11060469899976761753)
XLA Ops:
  6.6 2.2 cosine_convert_fusion
  8.8 0.7 concatenate.69
  9.5 0.2 tile.10
  9.7 3.8 %tile.11 = bf16[1179648]{0:T(1024)(128)(2,1)} reshape(bf16[1024,1152]{1,0:T(8,128)(2,1)S(1)} %tile.10) | data formatting | bytes 4718592 | tf_op jit(solution)/shard_map/tile | solution.py:14
  13.5 1.7 slice-done
  15.2 6.4 %reshape.232 = bf16[1024,1151]{1,0:T(8,128)(2,1)} reshape(bf16[1178624]{0:T(1024)(128)(2,1)S(1)} %slice-done) | data formatting | bytes 4714496 | tf_op jit(solution)/shard_map/reshape | solution.py:14
  21.5 10.3 %fusion.6 = f32[2560,256]{1,0:T(8,128)S(1)} fusion(bf16[2560,1024]{1,0:T(8,128)(2,1)} %bitcast.16, bf16[1024,1151]{1,0:T(8,128)(2,1)} %reshape.232, bf16[1024,128]{1,0:T(8,128)(2,1)S(1)} %get-tuple-element.16, bf16[1024,128]{1,0:T(8,128)(2,1)S(1)} %get-tuple-element.15), kind=kOutput, calls=%fused_computation.14 | convolution fusion | flops 6714556416 | bytes 10485760 | tf_op jit(solution)/shard_map/dot_general | solution.py:68
  31.9 0.5 fusion.17
  32.4 1.5 fusion
  33.9 0.5 fusion.1
  34.5 2.1 copy.11
  36.6 0.0 all-gather.2.cloned.1.call-update
  36.6 0.0 all-reduce.3.cloned.1.call-start
  36.6 6.8 %sort.17 = (s32[5120]{0:T(1024)}, s32[5120]{0:T(1024)S(1)}) sort(s32[5120]{0:T(1024)S(1)} %copy-done, s32[5120]{0:T(1024)S(1)} %iota.22), dimensions={0}, to_apply=%region_0.0 | sort | flops 66560 | bytes 81920 | tf_op jit(solution)/shard_map/jit(argsort)/sort | solution.py:58
  43.4 6.4 %gather_fusion = s32[1024]{0:T(1024)S(1)} fusion(s32[5120]{0:T(1024)S(1)} %get-tuple-element.6, s32[1024]{0:T(1024)S(1)} %broadcast_clamp_fusion.1), kind=kCustom, calls=%fused_computation | custom fusion | bytes 12288 | tf_op jit(solution)/shard_map/jit(_take)/gather | solution.py:60
  49.9 140.1 %all-gather.2.cloned.1.call-done = bf16[4,5120,256]{2,0,1:T(4,128)(2,1)} async-done(((bf16[4,640,256]{2,0,1:T(4,128)(2,1)}), bf16[4,5120,256]{2,0,1:T(4,128)(2,1)}) %all-gather.2.cloned.1.call-update) | async-done | bytes 10485776 | tf_op jit(solution)/shard_map/all_gather | solution.py:72
  190.0 7.9 %gather_fusion.1 = bf16[1024,4,256]{2,1,0:T(4,128)(2,1)S(1)} fusion(bf16[4,5120,256]{2,0,1:T(4,128)(2,1)} %all-gather.2.cloned.1.call-done, s32[1024]{0:T(1024)S(1)} %broadcast_clamp_fusion), kind=kCustom, calls=%fused_computation.1 | custom fusion | bytes 4198400 | tf_op jit(solution)/shard_map/jit(_take)/gather | solution.py:74
  197.9 6.5 %select_bitcast_fusion = bf16[4,1024,256]{2,0,1:T(4,128)(2,1)S(1)} fusion(bf16[1024,4,256]{2,1,0:T(4,128)(2,1)S(1)} %gather_fusion.1, pred[1024]{0:T(1024)(128)(4,1)S(1)} %get-tuple-element.12, pred[1024]{0:T(1024)(128)(4,1)S(1)} %get-tuple-element.11), kind=kLoop, calls=%fused_computation.9 | loop fusion | flops 2097152 | bytes 4196352 | tf_op jit(solution)/shard_map/jit(_where)/select_n | solution.py:75
  204.4 0.5 slice_convert_fusion.1
  204.9 0.5 multiply_add_fusion
  205.5 2.2 maximum_reduce_fusion
  207.7 0.0 all-reduce.3.cloned.1.call-update
  207.7 31.7 %all-reduce.3.cloned.1.call-done = f32[512,256]{1,0:T(8,128)} async-done(((f32[512,256]{1,0:T(8,128)}), f32[512,256]{1,0:T(8,128)}) %all-reduce.3.cloned.1.call-update) | async-done | bytes 524304 | tf_op jit(solution)/shard_map/psum | solution.py:78
  239.4 1.9 broadcast_multiply_fusion
  (16 shorter events, 0.1 us)
Async XLA Ops:
  6.5 183.4 %all-gather.2.cloned.1.call-start = ((), (), s32[]{:S(2)}) async-start(), calls=%async_computation | async-start | bytes 11796480 | tf_op jit(solution)/shard_map/all_gather | solution.py:72
  13.5 1.7 slice-start
  34.4 2.2 copy-start
  34.5 9.0 %copy-start.1 = (s32[512,2]{0,1:T(2,128)S(1)}, s32[512,2]{0,1:T(2,128)}, u32[]{:S(2)}) copy-start(s32[512,2]{0,1:T(2,128)} %param.7) | copy-start | bytes 12292
  36.6 202.8 %all-reduce.3.cloned.1.call-start = ((), (), s32[]{:S(2)}) async-start(), calls=%async_computation.1 | async-start | bytes 1048576 | tf_op jit(solution)/shard_map/psum | solution.py:78
Sparse Core Ops, SparseCore 0:
  36.7 153.2 all-gather.1
  207.8 31.5 all-reduce.2
where the time goes:
time: 248 us
  waiting for transfers between devices  172 us (69%)
  local copies, waits for them, and re-layouts  29.1 us (12%)
  other arithmetic  21.8 us (9%)
  between operations  13.5 us (5%)
  matrix products  11.8 us (5%)
    all_gather x1, waiting for transfers between devices, local(): part_rows = lax.all_gather(whitened, 'chan', axis=1, tiled=True)  140 us
    psum x1, waiting for transfers between devices, local(): summed = lax.psum(stacked, 'tm')  31.7 us
    dot_general x1, matrix products, local(): spectrum = jnp.dot(filtered, dft_table, preferred_element_type=jnp.float32)  10.3 us
    gather x1, local copies, waits for them, and re-layouts, local(): jnp.take(part_rows, jnp.clip(wanted_ids, 0, part_rows.shape[1] - 1), axis=1)  7.92 us
    sort x1, other arithmetic, local(): rows_of = jnp.argsort(recorder_channel, stable=True)  6.76 us
    select_n x1, other arithmetic, local(): chosen = jnp.where(inside[None, :, None], taken, empty)  6.46 us
    gather x1, local copies, waits for them, and re-layouts, local(): wanted_ids = jnp.take(rows_of, endpoints)  6.37 us
    reshape x1, local copies, waits for them, and re-layouts, make_fir(): jnp.tile(padded, length)[:length * (period - 1)].reshape(length, period - 1)  6.35 us
  transfers between devices with their start and end apart: 2, of which 2 were waited for; matrix products, arithmetic and copies ran while one was open for 5% of the time, Pallas kernels for 0%

commit v1 on v0

--- a/solution.py
+++ b/solution.py
@@ -5,6 +5,24 @@
 
 NB = 128
 SMOOTH = 4
+
+
+def in_order(parts, dim):
+    lengths = list(parts.shape[1:])
+    lengths[dim] *= parts.shape[0]
+    return jnp.moveaxis(parts, 0, dim).reshape(lengths)
+
+
+def grow_blocks(x, axis):
+    peers = lax.axis_size(axis)
+    blocks = x[None]
+    for level in range(peers.bit_length() - 1):
+        bit = 1 << level
+        partner_block = lax.ppermute(blocks, axis, [(i, i ^ bit) for i in range(peers)])
+        both = jnp.stack([blocks, partner_block])
+        upper = lax.axis_index(axis) >> level & 1
+        blocks = jnp.where(upper == 0, both, both[::-1]).reshape(-1, *x.shape)
+    return blocks
 
 
 def make_fir(fir_taps, length):
@@ -69,7 +87,7 @@
     whitened = whiten(spectrum, smoother).reshape(windows, ch_dev, 2 * NB)
     pair_count = pairs.shape[0]
     empty = jnp.zeros((windows, 2 * pair_count, 2 * NB), jnp.bfloat16)
-    part_rows = lax.all_gather(whitened, "chan", axis=1, tiled=True)
+    part_rows = in_order(grow_blocks(whitened, "chan"), 1)
     inside = (wanted_ids >= 0) & (wanted_ids < part_rows.shape[1])
     taken = jnp.take(part_rows, jnp.clip(wanted_ids, 0, part_rows.shape[1] - 1), axis=1)
     chosen = jnp.where(inside[None, :, None], taken, empty)

time: 248 us -> 464 us (1.87)
  waiting for transfers between devices: 172 us -> 331 us
  other arithmetic: 21.8 us -> 54.7 us
  local copies, waits for them, and re-layouts: 29.1 us -> 45.3 us
  starting transfers between devices: 0.04 us -> 7.3 us
    ppermute x0 -> x3, waiting for transfers between devices: none -> 297 us  [grow_blocks(): lax.ppermute(blocks, axis, [(i, i ^ bit) for i in range(peers)])]
    all_gather x1 -> x0, waiting for transfers between devices: 140 us -> none  [local(): part_rows = lax.all_gather(whitened, 'chan', axis=1, tiled=True)]
    select_n x0 -> x2, other arithmetic: none -> 16.1 us  [grow_blocks(): blocks = jnp.where(upper == 0, both, both[::-1]).reshape(-1, *x.shape)]
    another operation x1 -> x5, other arithmetic: 2.22 us -> 18.1 us  [the longest x4 15.9 us: grow_blocks(): both = jnp.stack([blocks, partner_block])]
    reshape x1 -> x2, local copies, waits for them, and re-layouts: 2.09 us -> 17.5 us  [the longest x1 14.6 us: in_order(): return jnp.moveaxis(parts, 0, dim).reshape(lengths)]
    ppermute x0 -> x3, starting transfers between devices: none -> 7.29 us  [grow_blocks(): lax.ppermute(blocks, axis, [(i, i ^ bit) for i in range(peers)])]
  transfers between devices with their start and end apart: 2 -> 4, of which waited for: 2 -> 4; matrix products, arithmetic and copies ran while one was open for 5% -> 3% of each run, Pallas kernels for 0% -> 0%
where the time goes in v1:
time: 464 us
  waiting for transfers between devices  331 us (71%)
  other arithmetic  54.7 us (12%)
  local copies, waits for them, and re-layouts  45.3 us (10%)
  between operations  13.5 us (3%)
  matrix products  11.8 us (3%)
  starting transfers between devices  7.3 us (2%)
    ppermute x3, waiting for transfers between devices, grow_blocks(): lax.ppermute(blocks, axis, [(i, i ^ bit) for i in range(peers)])  297 us
    psum x1, waiting for transfers between devices, local(): summed = lax.psum(stacked, 'tm')  34.3 us
    select_n x2, other arithmetic, grow_blocks(): blocks = jnp.where(upper == 0, both, both[::-1]).reshape(-1, *x.shape)  16.1 us
    another operation x4, other arithmetic, grow_blocks(): both = jnp.stack([blocks, partner_block])  15.9 us
    reshape x1, local copies, waits for them, and re-layouts, in_order(): return jnp.moveaxis(parts, 0, dim).reshape(lengths)  14.6 us
    dot_general x1, matrix products, local(): spectrum = jnp.dot(filtered, dft_table, preferred_element_type=jnp.float32)  10.3 us
  transfers between devices with their start and end apart: 4, of which 4 were waited for; matrix products, arithmetic and copies ran while one was open for 3% of the time, Pallas kernels for 0%

profile of v1, /device:TPU:0, one launch (start us, length us, event | category | flops | bytes accessed | tf_op | source)
XLA Modules:
  0.0 464.0 jit_solution(1699070462504247648)
XLA Ops:
  6.6 2.2 cosine_convert_fusion
  9.7 3.8 tile.11
  13.5 1.7 slice-done
  15.2 6.4 %reshape.241 = bf16[1024,1151]{1,0:T(8,128)(2,1)} reshape(bf16[1178624]{0:T(1024)(128)(2,1)S(1)} %slice-done) | data formatting | bytes 4714496 | tf_op jit(solution)/shard_map/reshape | solution.py:32
  21.5 10.3 %fusion.8 = f32[2560,256]{1,0:T(8,128)S(1)} fusion(bf16[2560,1024]{1,0:T(8,128)(2,1)} %bitcast.40, bf16[1024,1151]{1,0:T(8,128)(2,1)} %reshape.241, bf16[1024,128]{1,0:T(8,128)(2,1)S(1)} %get-tuple-element.18, bf16[1024,128]{1,0:T(8,128)(2,1)S(1)} %get-tuple-element.17), kind=kOutput, calls=%fused_computation.22 | convolution fusion | flops 6714556416 | bytes 10485760 | tf_op jit(solution)/shard_map/dot_general | solution.py:86
  35.5 3.0 collective-permute-start
  38.5 29.0 %collective-permute-done = bf16[1,4,640,256]{3,2,1,0:T(8,128)(2,1)S(1)} collective-permute-done((bf16[1,4,640,256]{3,2,1,0:T(8,128)(2,1)}, bf16[1,4,640,256]{3,2,1,0:T(8,128)(2,1)S(1)}, u32[]{:S(2)}, u32[]{:S(2)}) %collective-permute-start) | collective-permute-done | bytes 1310752 | tf_op jit(solution)/shard_map/ppermute | solution.py:21
  69.0 2.3 fusion.4
  71.3 1.8 collective-permute-start.1
  73.1 56.6 %collective-permute-done.1 = bf16[2,4,640,256]{3,2,1,0:T(8,128)(2,1)} collective-permute-done((bf16[2,4,640,256]{3,2,1,0:T(8,128)(2,1)}, bf16[2,4,640,256]{3,2,1,0:T(8,128)(2,1)}, u32[]{:S(2)}, u32[]{:S(2)}) %collective-permute-start.1) | collective-permute-done | bytes 2621472 | tf_op jit(solution)/shard_map/ppermute | solution.py:21
  129.6 2.2 pad_maximum_fusion.1
  133.0 2.9 copy.11
  136.8 2.5 collective-permute-start.2
  139.3 6.8 %sort.17 = (s32[5120]{0:T(1024)}, s32[5120]{0:T(1024)S(1)}) sort(s32[5120]{0:T(1024)S(1)} %copy-done.1, s32[5120]{0:T(1024)S(1)} %iota.22), dimensions={0}, to_apply=%region_0.0 | sort | flops 66560 | bytes 81920 | tf_op jit(solution)/shard_map/jit(argsort)/sort | solution.py:76
  146.1 6.2 %gather_fusion = s32[1024]{0:T(1024)S(1)} fusion(s32[5120]{0:T(1024)S(1)} %get-tuple-element.6, s32[1024]{0:T(1024)S(1)} %broadcast_clamp_fusion.1), kind=kCustom, calls=%fused_computation | custom fusion | bytes 12288 | tf_op jit(solution)/shard_map/jit(_take)/gather | solution.py:78
  152.3 211.4 %collective-permute-done.2 = bf16[4,4,640,256]{3,2,0,1:T(8,128)(2,1)} collective-permute-done((bf16[4,4,640,256]{3,2,0,1:T(8,128)(2,1)}, bf16[4,4,640,256]{3,2,0,1:T(8,128)(2,1)}, u32[]{:S(2)}, u32[]{:S(2)}) %collective-permute-start.2) | collective-permute-done | bytes 5242912 | tf_op jit(solution)/shard_map/ppermute | solution.py:21
  363.7 9.9 %pad_maximum_fusion = bf16[2,4,4,640,256]{4,3,1,0,2:T(8,128)(2,1)} fusion(bf16[1,4,4,640,256]{4,3,1,0,2:T(8,128)(2,1)} %bitcast.12, bf16[1,4,4,640,256]{4,3,2,1,0:T(8,128)(2,1)} %bitcast.32), kind=kLoop, calls=%fused_computation.3 | loop fusion | flops 20971520 | bytes 20971520 | tf_op jit(solution)/shard_map/stack | solution.py:22
  373.6 15.0 %reverse_select_fusion = bf16[2,4,4,640,256]{4,3,1,0,2:T(8,128)(2,1)} fusion(bf16[2,4,4,640,256]{4,3,1,0,2:T(8,128)(2,1)} %pad_maximum_fusion, pred[]{:T(512)S(6)} %eq.11), kind=kLoop, calls=%fused_computation.2 | loop fusion | flops 5242880 | bytes 20971520 | tf_op jit(solution)/shard_map/jit(_where)/select_n | solution.py:24
  388.6 14.6 %copy.13 = bf16[4,5120,256]{2,0,1:T(4,128)(2,1)} copy(bf16[4,5120,256]{2,1,0:T(8,128)(2,1)} %bitcast.33) | data formatting | bytes 20971520 | tf_op jit(solution)/shard_map/reshape | solution.py:13
  403.2 7.9 %gather_fusion.1 = bf16[1024,4,256]{2,1,0:T(4,128)(2,1)S(1)} fusion(bf16[4,5120,256]{2,0,1:T(4,128)(2,1)} %copy.13, s32[1024]{0:T(1024)S(1)} %broadcast_clamp_fusion), kind=kCustom, calls=%fused_computation.1 | custom fusion | bytes 4198400 | tf_op jit(solution)/shard_map/jit(_take)/gather | solution.py:92
  411.1 6.5 %select_bitcast_fusion = bf16[4,1024,256]{2,0,1:T(4,128)(2,1)S(1)} fusion(bf16[1024,4,256]{2,1,0:T(4,128)(2,1)S(1)} %gather_fusion.1, pred[1024]{0:T(1024)(128)(4,1)S(1)} %get-tuple-element.14, pred[1024]{0:T(1024)(128)(4,1)S(1)} %get-tuple-element.13), kind=kLoop, calls=%fused_computation.15 | loop fusion | flops 2097152 | bytes 4196352 | tf_op jit(solution)/shard_map/jit(_where)/select_n | solution.py:93
  418.7 2.2 maximum_reduce_fusion
  420.9 34.3 %all-reduce.3.cloned.1.call-done = f32[512,256]{1,0:T(8,128)} async-done(((f32[512,256]{1,0:T(8,128)}), f32[512,256]{1,0:T(8,128)}) %all-reduce.3.cloned.1.call-update) | async-done | bytes 524304 | tf_op jit(solution)/shard_map/psum | solution.py:96
  455.3 1.9 broadcast_multiply_fusion
  (28 shorter events, 9.2 us)
Async XLA Ops:
  6.5 448.7 %all-reduce.3.cloned.1.call-start = ((), (), s32[]{:S(2)}) async-start(), calls=%async_computation | async-start | bytes 1048576 | tf_op jit(solution)/shard_map/psum | solution.py:96
  13.5 1.7 slice-start
  35.5 32.0 %collective-permute-start = (bf16[1,4,640,256]{3,2,1,0:T(8,128)(2,1)}, bf16[1,4,640,256]{3,2,1,0:T(8,128)(2,1)S(1)}, u32[]{:S(2)}, u32[]{:S(2)}) collective-permute-start(bf16[1,4,640,256]{3,2,1,0:T(8,128)(2,1)} %bitcast.5), channel_id=1, source_target_pairs={{0,1},{1,0},{2,3},{3,2},{4,5},{5,4},{6,7},{7,6},{8,9},{9,8},{10,11... | collective-permute-start | bytes 3932168 | tf_op jit(solution)/shard_map/ppermute | solution.py:21
  71.3 58.4 %collective-permute-start.1 = (bf16[2,4,640,256]{3,2,1,0:T(8,128)(2,1)}, bf16[2,4,640,256]{3,2,1,0:T(8,128)(2,1)}, u32[]{:S(2)}, u32[]{:S(2)}) collective-permute-start(bf16[2,4,640,256]{3,2,1,0:T(8,128)(2,1)} %get-tuple-element.10), channel_id=1, source_target_pairs={{0,2},{1,3},{2,0},{3,1},{4,6},{5,7},{6,4},{7,5},{8,10},{9,11},{10,... | collective-permute-start | bytes 7864328 | tf_op jit(solution)/shard_map/ppermute | solution.py:21
  132.9 3.9 copy-start
  132.9 6.4 %copy-start.1 = (s32[5120]{0:T(1024)S(1)}, s32[5120]{0:T(1024)}, u32[]{:S(2)}) copy-start(s32[5120]{0:T(1024)} %param.6) | copy-start | bytes 61444
  132.9 13.1 %copy-start.2 = (s32[512,2]{0,1:T(2,128)S(1)}, s32[512,2]{0,1:T(2,128)}, u32[]{:S(2)}) copy-start(s32[512,2]{0,1:T(2,128)} %param.7) | copy-start | bytes 12292
  136.8 226.9 %collective-permute-start.2 = (bf16[4,4,640,256]{3,2,0,1:T(8,128)(2,1)}, bf16[4,4,640,256]{3,2,0,1:T(8,128)(2,1)}, u32[]{:S(2)}, u32[]{:S(2)}) collective-permute-start(bf16[4,4,640,256]{3,2,0,1:T(8,128)(2,1)} %copy.11), channel_id=1, source_target_pairs={{0,4},{1,5},{2,6},{3,7},{4,0},{5,1},{6,2},{7,3},{8,12},{9,13},{10,... | collective-permute-start | bytes 15728648 | tf_op jit(solution)/shard_map/ppermute | solution.py:21
Sparse Core Ops, SparseCore 0:
  421.0 34.1 all-reduce.2
